TPU v7x, 512 devices: a whole 4x4x16 slice. The times are simulated.
512 devices in a mesh: seq: 32 (over y, x, core), head: 16 (over z).
Axes of the slice: x: 4, y: 4, z: 16, core: 2. Of those that a mesh axis runs over, the one named last changes fastest.
Arguments:
- values: bfloat16 [16384, 8192], P('seq', 'head'), may hold values from -6 to 6
- group_keys: bfloat16 [16384, 8, 128], P(('seq', 'head')), may hold values from -0.5 to 0.5
- group_queries: bfloat16 [16384, 8, 128], P(('seq', 'head')), may hold values from -0.16992188 to 0.16992188
- level_table: int32 [128, 20], P('head'), may hold values from 1 to 4
- window_index: int32 [1], replicated, may hold values from 0 to 15
- prior_states: bfloat16 [4, 128, 64, 128], P(None, 'head'), may hold values from -100 to 100
- cotangent: bfloat16 [16384, 8192], P('seq', 'head'), may hold values from -6 to 6
Outputs:
- mixer_out: bfloat16 [16384, 8192], P('seq', 'head')
- grad_values: bfloat16 [16384, 8192], P('seq', 'head')
- grad_keys: float32 [16384, 8, 128], P(('seq', 'head'))
- grad_queries: float32 [16384, 8, 128], P(('seq', 'head'))
- grad_prior: float32 [4, 128, 64, 128], P(None, 'head')
All inputs are finite; a program needn't handle non-finite values.
Results may differ from a plain program's by a relative error of at most 0.015.
Values may be sent and summed in bfloat16 or wider, within the bound.
A program may use at most 64 MiB of HBM per device.

v0:
```python
import jax
import jax.numpy as jnp
from jax import lax
from jax.experimental import pallas as pl
from jax.experimental.pallas import tpu as pltpu
from jax.sharding import PartitionSpec as P

HEADS = 128
GROUPS = 8
NS = 32
NH = 16
TOK = 512
HP = 512
LOC = 8
N = 128
BF = jnp.bfloat16
F32 = jnp.float32
MESH = pl.DeviceIdType.MESH

NN = (((1,), (0,)), ((), ()))
NT = (((1,), (1,)), ((), ()))
TN = (((0,), (0,)), ((), ()))


def mm(a, b, dims=NN):
    return lax.dot_general(a, b, dims, preferred_element_type=F32)


def root(level):
    return float(2.0 ** (-max(level - 1, 0) / 2))


def hops():
    rel = [(dy, dx, dc) for dy in range(4) for dx in range(4) for dc in range(2)]
    rel.remove((0, 0, 0))
    near = lambda a: min(a, 4 - a)
    rel.sort(key=lambda r: -(near(r[0]) + near(r[1])))
    return rel


def kernel(
    v_hbm, k_hbm, q_hbm, table, window, prior_hbm, c_hbm,
    mix_hbm, gv_hbm, gk_hbm, gq_hbm, tot_hbm, prior_w_hbm,
    v, c, kraw, qraw, prior, vt, ct, kq_send, kq, factor, factor_t,
    g_diag, g_8, g_9, sa_send, sa_recv, io_send, io_recv, tot_send, tot_recv,
    mix, gval, grad, mate_send, mate_recv, out_send, back, outs, rows_out, prior_w,
    local_sem, gat_send, gat_recv, fwd_send, sa_ss, sa_rs, io_ss, io_rs, tot_ss, tot_rs,
    mt_ss, mt_rs, bk_ss, bk_rs,
):
    me = lax.axis_index("seq")
    z = lax.axis_index("head")
    pair = lax.div(z, 2)
    odd = lax.rem(z, 2)
    sgn = 2 * odd - 1
    mate = z - sgn
    ring = lambda i: lax.rem(i + 2 * NH, NH)
    core, xx, yy = lax.rem(me, 2), lax.rem(lax.div(me, 2), 4), lax.div(me, 8)

    def seq_of(rel):
        dy, dx, dc = rel
        return lax.rem(yy + dy, 4) * 8 + lax.rem(xx + dx, 4) * 2 + lax.rem(core + dc, 2)

    relative = hops()
    near_z = [ring(z + sgn * j) for j in range(1, 8)]
    far_z = [ring(z - sgn * j) for j in (2, 4, 6)]

    loads = [
        pltpu.make_async_copy(k_hbm, kraw, local_sem.at[0]),
        pltpu.make_async_copy(q_hbm, qraw, local_sem.at[1]),
        pltpu.make_async_copy(v_hbm, v, local_sem.at[2]),
        pltpu.make_async_copy(c_hbm, c, local_sem.at[3]),
        pltpu.make_async_copy(prior_hbm.at[:, pl.ds(pl.multiple_of(me * 16, 16), 16), :], prior, local_sem.at[4]),
    ]
    for load in loads:
        load.start()

    barrier = pltpu.get_barrier_semaphore()
    for other in near_z + far_z + [mate]:
        pl.semaphore_signal(barrier, inc=1, device_id={"head": other}, device_id_type=MESH)
    for rel in relative:
        pl.semaphore_signal(barrier, inc=1, device_id={"seq": seq_of(rel)}, device_id_type=MESH)

    out_row = lax.broadcasted_iota(jnp.int32, (256, 256), 0)
    in_row = lax.broadcasted_iota(jnp.int32, (256, 256), 1)
    pick = (in_row == (out_row & 31) * 8 + (out_row >> 5)).astype(F32).astype(BF)
    loads[0].wait()
    k_sorted = mm(pick, kraw[...]).astype(BF)
    loads[1].wait()
    q_sorted = mm(pick, qraw[...]).astype(BF)
    for g in range(GROUPS):
        kq_send[g, 0:32, :] = k_sorted[32 * g : 32 * g + 32, :]
        kq_send[g, 32:64, :] = q_sorted[32 * g : 32 * g + 32, :]
    kq[z] = kq_send[pair]

    weight = lambda h, l: table[h, l].astype(F32) * root(l)
    row = lax.broadcasted_iota(jnp.int32, (128, 128), 0)
    col = lax.broadcasted_iota(jnp.int32, (128, 128), 1)
    spread = row ^ col
    for h in range(LOC):
        grid = jnp.full((128, 128), weight(h, 7), F32)
        for l in range(6, -1, -1):
            grid = jnp.where(spread < (1 << l), weight(h, l), grid)
        factor[h] = jnp.where(row >= col, grid, 0.0)
        factor_t[h] = jnp.where(col >= row, grid, 0.0)

    lane = lax.broadcasted_iota(jnp.int32, (1, HP), 1) >> 6

    def lanes_of(level):
        w = jnp.zeros((1, HP), F32)
        for h in range(LOC):
            w = jnp.where(lane == h, weight(h, level), w)
        return w

    w8, w9 = lanes_of(8), lanes_of(9)
    low_half = lax.broadcasted_iota(jnp.int32, (128, 128), 1) < 64

    def both(ref, i, pr):
        tile = ref[128 * i : 128 * i + 128, 128 * pr : 128 * pr + 128]
        zero = jnp.zeros_like(tile)
        return jnp.concatenate([jnp.where(low_half, tile, zero), jnp.where(low_half, zero, tile)], axis=0)

    loads[2].wait()
    loads[3].wait()
    vt[...] = v[...].T
    ct[...] = c[...].T

    def wide_grads():
        g_9[...] = mm((c[256:512, :].astype(F32) * w9).astype(BF), v[0:256, :], NT).astype(BF)
        for i in range(2):
            at = 256 * i
            g_8[i] = mm((c[at + 128 : at + 256, :].astype(F32) * w8).astype(BF), v[at : at + 128, :], NT).astype(BF)

    def diagonal_grads(i):
        total = jnp.zeros((128, 128), F32)
        for pr in range(4):
            raw = mm(both(c, i, pr), v[128 * i : 128 * i + 128, 128 * pr : 128 * pr + 128], NT)
            total = total + factor[2 * pr] * raw[:128] + factor[2 * pr + 1] * raw[128:]
        g_diag[i] = total.astype(BF)

    pl.semaphore_wait(barrier, 11 + 31)

    def gather_copy(block, to):
        return pltpu.make_async_remote_copy(
            src_ref=kq_send.at[block], dst_ref=kq.at[z], send_sem=gat_send.at[block], recv_sem=gat_recv.at[z],
            device_id={"head": to}, device_id_type=MESH,
        )

    opposite = lax.rem(pair + 4, 8)
    gathers = [gather_copy(opposite, 2 * opposite + 1 - odd)]
    for k in (3, 2, 1):
        right, left = lax.rem(pair + k, 8), lax.rem(pair + 8 - k, 8)
        gathers += [gather_copy(right, 2 * right), gather_copy(left, 2 * left + 1)]
    gathers.append(gather_copy(pair, mate))
    for copy in gathers:
        copy.start()

    wide_grads()
    for i in range(4):
        diagonal_grads(i)

    forwards = []
    for j in range(7):
        src = near_z[j]
        pltpu.make_async_remote_copy(
            src_ref=kq.at[src], dst_ref=kq.at[src], send_sem=gat_send.at[0], recv_sem=gat_recv.at[src],
            device_id={"head": mate}, device_id_type=MESH,
        ).wait_recv()
        forward = pltpu.make_async_remote_copy(
            src_ref=kq.at[src], dst_ref=kq.at[src], send_sem=fwd_send.at[j], recv_sem=gat_recv.at[src],
            device_id={"head": mate}, device_id_type=MESH,
        )
        forward.start()
        forwards.append(forward)
    for src in [mate] + [ring(mate - sgn * j) for j in range(1, 8)]:
        pltpu.make_async_remote_copy(
            src_ref=kq.at[src], dst_ref=kq.at[src], send_sem=gat_send.at[0], recv_sem=gat_recv.at[src],
            device_id={"head": mate}, device_id_type=MESH,
        ).wait_recv()

    keys = kq[:, 0:32, :].reshape(TOK, N)
    queries = kq[:, 32:64, :].reshape(TOK, N)

    sa_send[:, 0] = mm(vt[...], keys).astype(BF).reshape(NS, 16, N)
    sa_send[:, 1] = mm(ct[...], queries).astype(BF).reshape(NS, 16, N)

    def spread_out(src, dst, ss, rs, whole):
        copies = []
        for n, rel in enumerate(relative):
            to = seq_of(rel)
            copies.append(pltpu.make_async_remote_copy(
                src_ref=src if whole else src.at[to], dst_ref=dst.at[me], send_sem=ss.at[n], recv_sem=rs.at[me],
                device_id={"seq": to}, device_id_type=MESH,
            ))
        for copy in copies:
            copy.start()
        return copies

    def arrive(dst, ss, rs):
        for rel in relative:
            frm = seq_of(rel)
            pltpu.make_async_remote_copy(
                src_ref=dst.at[frm], dst_ref=dst.at[frm], send_sem=ss.at[0], recv_sem=rs.at[frm],
                device_id={"seq": frm}, device_id_type=MESH,
            ).wait_recv()

    sa_copies = spread_out(sa_send, sa_recv, sa_ss, sa_rs, False)
    sa_recv[me] = sa_send[me]

    def block(i):
        return slice(128 * i, 128 * i + 128)

    def inner_outputs():
        for i in range(4):
            q_i, k_i = queries[block(i)], keys[block(i)]
            score, score_t = mm(q_i, k_i, NT), mm(k_i, q_i, NT)
            for pr in range(4):
                cols = slice(128 * pr, 128 * pr + 128)
                w = jnp.concatenate([(factor[2 * pr] * score).astype(BF), (factor[2 * pr + 1] * score).astype(BF)], axis=1)
                mix[block(i), cols] = mm(w, both(v, i, pr))
                w = jnp.concatenate([(factor_t[2 * pr] * score_t).astype(BF), (factor_t[2 * pr + 1] * score_t).astype(BF)], axis=1)
                gval[block(i), cols] = mm(w, both(c, i, pr))
        for i in range(2):
            lo, hi = block(2 * i), block(2 * i + 1)
            mix[hi, :] += w8 * mm(mm(queries[hi], keys[lo], NT).astype(BF), v[lo, :])
            gval[lo, :] += w8 * mm(mm(keys[lo], queries[hi], NT).astype(BF), c[hi, :])
        lo, hi = slice(0, 256), slice(256, 512)
        mix[hi, :] += w9 * mm(mm(queries[hi], keys[lo], NT).astype(BF), v[lo, :])
        gval[lo, :] += w9 * mm(mm(keys[lo], queries[hi], NT).astype(BF), c[hi, :])

    def inner_grads():
        for i in range(4):
            gq = mm(g_diag[i], keys[block(i)])
            gk = mm(g_diag[i], queries[block(i)], TN)
            if i % 2 == 1:
                gq = gq + mm(g_8[i // 2], keys[block(i - 1)])
            else:
                gk = gk + mm(g_8[i // 2], queries[block(i + 1)], TN)
            if i >= 2:
                gq = gq + mm(g_9[128 * (i - 2) : 128 * (i - 1), :], keys[0:256])
            else:
                gk = gk + mm(g_9[:, 128 * i : 128 * (i + 1)], queries[256:512], TN)
            grad[4 * i : 4 * i + 4, 0:32] = gk.reshape(4, 32, N)
            grad[4 * i : 4 * i + 4, 32:64] = gq.reshape(4, 32, N)

    inner_grads()

    arrive(sa_recv, sa_ss, sa_rs)
    my_head = lax.div(me, 4)
    seq_w = [table[my_head, 10 + b].astype(F32) * root(10 + b) for b in range(5)]
    bit = lambda k: ((window[0] >> k) & 1).astype(F32)
    loads[4].wait()
    start = jnp.zeros((16, N), F32)
    for k in range(4):
        start = start + (table[my_head, 15 + k].astype(F32) * root(15 + k) * bit(k)) * prior[k].astype(F32)

    def sums(which):
        levels = [[sa_recv[j, which].astype(F32) for j in range(NS)]]
        for _ in range(5):
            last = levels[-1]
            levels.append([last[2 * j] + last[2 * j + 1] for j in range(len(last) // 2)])
        return levels

    levels = sums(0)
    flow = [start]
    for b in range(4, -1, -1):
        flow = [x for j, f in enumerate(flow) for x in (f, f + seq_w[b] * levels[b][2 * j])]
    for j in range(NS):
        io_send[j, 0] = flow[j].astype(BF)
    levels = sums(1)
    flow = [jnp.zeros((16, N), F32)]
    for b in range(4, -1, -1):
        flow = [x for j, f in enumerate(flow) for x in (f + seq_w[b] * levels[b][2 * j + 1], f)]
    for j in range(NS):
        io_send[j, 1] = flow[j].astype(BF)
    tot_send[...] = levels[5][0].astype(BF)

    io_copies = spread_out(io_send, io_recv, io_ss, io_rs, False)
    tot_copies = spread_out(tot_send, tot_recv, tot_ss, tot_rs, True)
    io_recv[me] = io_send[me]
    tot_recv[me] = tot_send[...]

    inner_outputs()

    arrive(io_recv, io_ss, io_rs)
    inflow = io_recv[:, 0].reshape(HP, N)
    outflow = io_recv[:, 1].reshape(HP, N)
    grad[:, 0:32] = grad[:, 0:32] + mm(v[...], outflow).reshape(NH, 32, N)
    grad[:, 32:64] = grad[:, 32:64] + mm(c[...], inflow).reshape(NH, 32, N)
    mate_send[...] = grad[...].astype(BF)

    mate_copies = []
    for j in range(7, -1, -1):
        rows = ring(mate - sgn * j)
        mate_copies.append(pltpu.make_async_remote_copy(
            src_ref=mate_send.at[rows], dst_ref=mate_recv.at[j], send_sem=mt_ss.at[j], recv_sem=mt_rs.at[j],
            device_id={"head": mate}, device_id_type=MESH,
        ))
    for copy in mate_copies:
        copy.start()

    def mate_arrive(j):
        pltpu.make_async_remote_copy(
            src_ref=mate_recv.at[j], dst_ref=mate_recv.at[j], send_sem=mt_ss.at[j], recv_sem=mt_rs.at[j],
            device_id={"head": mate}, device_id_type=MESH,
        ).wait_recv()

    back_copies = []
    for j in range(7, 0, -1):
        to = near_z[j - 1]
        mate_arrive(j)
        out_send[j] = (grad[to] + mate_recv[j].astype(F32)).astype(BF)
        copy = pltpu.make_async_remote_copy(
            src_ref=out_send.at[j], dst_ref=back.at[pair], send_sem=bk_ss.at[j], recv_sem=bk_rs.at[pair],
            device_id={"head": to}, device_id_type=MESH,
        )
        copy.start()
        back_copies.append(copy)
    mate_arrive(0)
    back[pair] = (grad[z] + mate_recv[0].astype(F32)).astype(BF)

    stores = []

    def store(src, dst):
        stores.append(pltpu.make_async_copy(src, dst, local_sem.at[5 + len(stores)]))
        stores[-1].start()

    outs[0] = (mix[...] + mm(queries, inflow, NT)).astype(BF)
    store(outs.at[0], mix_hbm)
    outs[1] = (gval[...] + mm(keys, outflow, NT)).astype(BF)
    store(outs.at[1], gv_hbm)
    for h in range(LOC):
        for k in range(4):
            prior_w[8 * k + h : 8 * k + h + 1, :] = jnp.full((1, N), weight(h, 15 + k) * bit(k), F32)
    store(prior_w, prior_w_hbm)
    arrive(tot_recv, tot_ss, tot_rs)
    store(tot_recv, tot_hbm)

    for k in range(1, 8):
        frm = lax.rem(pair + k, 8)
        pltpu.make_async_remote_copy(
            src_ref=back.at[frm], dst_ref=back.at[frm], send_sem=bk_ss.at[0], recv_sem=bk_rs.at[frm],
            device_id={"head": mate}, device_id_type=MESH,
        ).wait_recv()
    for g in range(GROUPS):
        rows_out[0, pl.ds(g, 32, stride=8), :] = back[g, 0:32].astype(F32)
        rows_out[1, pl.ds(g, 32, stride=8), :] = back[g, 32:64].astype(F32)
    store(rows_out.at[0], gk_hbm)
    store(rows_out.at[1], gq_hbm)

    for copy in gathers + forwards + sa_copies + io_copies + tot_copies + mate_copies + back_copies:
        copy.wait_send()
    for copy in stores:
        copy.wait()


def store_kernel(*refs):
    ins, outs, held, sems = refs[:6], refs[6:11], refs[11:18], refs[18]
    order = (4, 5, 0, 1, 2, 3)
    loads = [pltpu.make_async_copy(ins[i], held[i], sems.at[i]) for i in range(6)]
    for i in order:
        loads[i].start()
    loads[4].wait()
    loads[5].wait()
    tot, prior_w, gp = held[4], held[5], held[6]
    stores = []
    for k in range(4):
        for h in range(LOC):
            piece = tot[4 * h : 4 * h + 4].reshape(64, N).astype(F32)
            gp[k, 64 * h : 64 * h + 64, :] = prior_w[8 * k + h : 8 * k + h + 1, :] * piece
        stores.append(pltpu.make_async_copy(gp.at[k], outs[4].at[k], sems.at[6 + k]))
        stores[-1].start()
    for i in range(4):
        loads[i].wait()
        stores.append(pltpu.make_async_copy(held[i], outs[i], sems.at[10 + i]))
        stores[-1].start()
    for copy in stores:
        copy.wait()


def per_device(values, group_keys, group_queries, level_table, window_index, prior_states, cotangent):
    hbm = pl.BlockSpec(memory_space=pltpu.HBM)
    smem = pl.BlockSpec(memory_space=pltpu.SMEM)
    dma = pltpu.SemaphoreType.DMA
    wide, narrow = jax.ShapeDtypeStruct((TOK, HP), BF), jax.ShapeDtypeStruct((256, N), F32)
    parts = pl.pallas_call(
        kernel,
        out_shape=(
            wide, wide, narrow, narrow,
            jax.ShapeDtypeStruct((NS, 16, N), BF),
            jax.ShapeDtypeStruct((32, N), F32),
        ),
        in_specs=[hbm, hbm, hbm, smem, smem, hbm, hbm],
        out_specs=(hbm,) * 6,
        scratch_shapes=[
            pltpu.VMEM((TOK, HP), BF),
            pltpu.VMEM((TOK, HP), BF),
            pltpu.VMEM((256, N), BF),
            pltpu.VMEM((256, N), BF),
            pltpu.VMEM((4, 16, N), BF),
            pltpu.VMEM((HP, TOK), BF),
            pltpu.VMEM((HP, TOK), BF),
            pltpu.VMEM((GROUPS, 64, N), BF),
            pltpu.VMEM((NH, 64, N), BF),
            pltpu.VMEM((LOC, 128, 128), F32),
            pltpu.VMEM((LOC, 128, 128), F32),
            pltpu.VMEM((4, 128, 128), BF),
            pltpu.VMEM((2, 128, 128), BF),
            pltpu.VMEM((256, 256), BF),
            pltpu.VMEM((NS, 2, 16, N), BF),
            pltpu.VMEM((NS, 2, 16, N), BF),
            pltpu.VMEM((NS, 2, 16, N), BF),
            pltpu.VMEM((NS, 2, 16, N), BF),
            pltpu.VMEM((16, N), BF),
            pltpu.VMEM((NS, 16, N), BF),
            pltpu.VMEM((TOK, HP), F32),
            pltpu.VMEM((TOK, HP), F32),
            pltpu.VMEM((NH, 64, N), F32),
            pltpu.VMEM((NH, 64, N), BF),
            pltpu.VMEM((8, 64, N), BF),
            pltpu.VMEM((8, 64, N), BF),
            pltpu.VMEM((GROUPS, 64, N), BF),
            pltpu.VMEM((2, TOK, HP), BF),
            pltpu.VMEM((2, 256, N), F32),
            pltpu.VMEM((32, N), F32),
            dma((11,)),
            dma((GROUPS,)),
            dma((NH,)),
            dma((7,)),
            dma((NS,)),
            dma((NS,)),
            dma((NS,)),
            dma((NS,)),
            dma((NS,)),
            dma((NS,)),
            dma((8,)),
            dma((8,)),
            dma((8,)),
            dma((8,)),
        ],
        compiler_params=pltpu.CompilerParams(
            collective_id=0, has_side_effects=True, vmem_limit_bytes=62 * 1024 * 1024
        ),
    )(
        values,
        group_keys.reshape(256, N),
        group_queries.reshape(256, N),
        level_table,
        window_index,
        prior_states.reshape(4, HP, N),
        cotangent,
    )
    outs = pl.pallas_call(
        store_kernel,
        out_shape=(wide, wide, narrow, narrow, jax.ShapeDtypeStruct((4, HP, N), F32)),
        in_specs=[hbm] * 6,
        out_specs=(hbm,) * 5,
        scratch_shapes=[
            pltpu.VMEM((TOK, HP), BF),
            pltpu.VMEM((TOK, HP), BF),
            pltpu.VMEM((256, N), F32),
            pltpu.VMEM((256, N), F32),
            pltpu.VMEM((NS, 16, N), BF),
            pltpu.VMEM((32, N), F32),
            pltpu.VMEM((4, HP, N), F32),
            dma((14,)),
        ],
        compiler_params=pltpu.CompilerParams(vmem_limit_bytes=62 * 1024 * 1024),
    )(*parts)
    mixer_out, grad_values, grad_keys, grad_queries, grad_prior = outs
    return (
        mixer_out,
        grad_values,
        grad_keys.reshape(32, GROUPS, N),
        grad_queries.reshape(32, GROUPS, N),
        grad_prior.reshape(4, LOC, 64, N),
    )


def solution(mesh):
    rows = P(("seq", "head"), None, None)
    return jax.shard_map(
        per_device,
        mesh=mesh,
        in_specs=(P("seq", "head"), rows, rows, P("head", None), P(), P(None, "head", None, None), P("seq", "head")),
        out_specs=(P("seq", "head"), P("seq", "head"), rows, rows, P(None, "head", None, None)),
        check_vma=False,
    )
```

profile of v0, /device:TPU:8, one launch (start us, length us, event | category | flops | bytes accessed | tf_op | source)
XLA Modules:
  0.0 58.7 jit_solution(17936171727245343199)
XLA Ops:
  1.3 55.0 %shard_map.110 = (bf16[512,512]{1,0:T(8,128)(2,1)}, bf16[512,512]{1,0:T(8,128)(2,1)}, f32[256,128]{1,0:T(8,128)}, f32[256,128]{1,0:T(8,128)}, bf16[32,16,128]{2,1,0:T(8,128)(2,1)}, /*index=5*/f32[32,128]{1,0:T(8,128)}) custom-call(bf16[512,512]{1,0:T(8,128)(2,1)} %v_hbm.1, bf16[256,128]{1,0:T(8,128)(2,1)} %bitcast.7, bf16[256,128]{1,0:T(8,128)(2,1)} %bitcast.8, ...), custom_call_target="tpu_custom_call" | custom-call | tf_op jit(solution)/shard_map/pallas_call | solution.py:385
  56.2 2.4 %shard_map.111 = (bf16[512,512]{1,0:T(8,128)(2,1)}, bf16[512,512]{1,0:T(8,128)(2,1)}, f32[256,128]{1,0:T(8,128)}, f32[256,128]{1,0:T(8,128)}, f32[4,512,128]{2,1,0:T(8,128)}) custom-call(bf16[512,512]{1,0:T(8,128)(2,1)} %get-tuple-element.16.refs_0_, bf16[512,512]{1,0:T(8,128)(2,1)} %get-tuple-element.17.refs_1_, f32[256,128]{1,0:T(8,128)} %get-tuple-element.18.refs_2_, ...), custom_call_target="tpu_custom_call" | custom-call | tf_op jit(solution)/shard_map/pallas_call | solution.py:452
where the time goes:
time: 58.9 us; the launch traced here: 58.7 us
  Pallas kernels  57.4 us (97%)
  between operations  1.29 us (2%)
    pallas_call x1, Pallas kernels, per_device(): pl.pallas_call(kernel, out_shape=(wide, wide, narrow, narrow, jax.ShapeDt...  55 us
    pallas_call x1, Pallas kernels, per_device(): pl.pallas_call(store_kernel, out_shape=(wide, wide, narrow, narrow, jax.S...  2.44 us

commit v1 on v0

--- a/solution.py
+++ b/solution.py
@@ -39,9 +39,9 @@
 
 
 def kernel(
-    v_hbm, k_hbm, q_hbm, table, window, prior_hbm, c_hbm,
+    v_hbm, k_hbm, q_hbm, table_hbm, window_hbm, prior_hbm, c_hbm,
     mix_hbm, gv_hbm, gk_hbm, gq_hbm, tot_hbm, prior_w_hbm,
-    v, c, kraw, qraw, prior, vt, ct, kq_send, kq, factor, factor_t,
+    table, window, v, c, kraw, qraw, prior, vt, ct, kq_send, kq, factor, factor_t,
     g_diag, g_8, g_9, sa_send, sa_recv, io_send, io_recv, tot_send, tot_recv,
     mix, gval, grad, mate_send, mate_recv, out_send, back, outs, rows_out, prior_w,
     local_sem, gat_send, gat_recv, fwd_send, sa_ss, sa_rs, io_ss, io_rs, tot_ss, tot_rs,
@@ -64,21 +64,23 @@
     near_z = [ring(z + sgn * j) for j in range(1, 8)]
     far_z = [ring(z - sgn * j) for j in (2, 4, 6)]
 
+    barrier = pltpu.get_barrier_semaphore()
+    for other in near_z + far_z + [mate]:
+        pl.semaphore_signal(barrier, inc=1, device_id={"head": other}, device_id_type=MESH)
+    for rel in relative:
+        pl.semaphore_signal(barrier, inc=1, device_id={"seq": seq_of(rel)}, device_id_type=MESH)
+
     loads = [
         pltpu.make_async_copy(k_hbm, kraw, local_sem.at[0]),
         pltpu.make_async_copy(q_hbm, qraw, local_sem.at[1]),
         pltpu.make_async_copy(v_hbm, v, local_sem.at[2]),
         pltpu.make_async_copy(c_hbm, c, local_sem.at[3]),
         pltpu.make_async_copy(prior_hbm.at[:, pl.ds(pl.multiple_of(me * 16, 16), 16), :], prior, local_sem.at[4]),
+        pltpu.make_async_copy(table_hbm, table, local_sem.at[11]),
+        pltpu.make_async_copy(window_hbm, window, local_sem.at[12]),
     ]
     for load in loads:
         load.start()
-
-    barrier = pltpu.get_barrier_semaphore()
-    for other in near_z + far_z + [mate]:
-        pl.semaphore_signal(barrier, inc=1, device_id={"head": other}, device_id_type=MESH)
-    for rel in relative:
-        pl.semaphore_signal(barrier, inc=1, device_id={"seq": seq_of(rel)}, device_id_type=MESH)
 
     out_row = lax.broadcasted_iota(jnp.int32, (256, 256), 0)
     in_row = lax.broadcasted_iota(jnp.int32, (256, 256), 1)
@@ -92,6 +94,7 @@
         kq_send[g, 32:64, :] = q_sorted[32 * g : 32 * g + 32, :]
     kq[z] = kq_send[pair]
 
+    loads[5].wait()
     weight = lambda h, l: table[h, l].astype(F32) * root(l)
     row = lax.broadcasted_iota(jnp.int32, (128, 128), 0)
     col = lax.broadcasted_iota(jnp.int32, (128, 128), 1)
@@ -249,6 +252,7 @@
     seq_w = [table[my_head, 10 + b].astype(F32) * root(10 + b) for b in range(5)]
     bit = lambda k: ((window[0] >> k) & 1).astype(F32)
     loads[4].wait()
+    loads[6].wait()
     start = jnp.zeros((16, N), F32)
     for k in range(4):
         start = start + (table[my_head, 15 + k].astype(F32) * root(15 + k) * bit(k)) * prior[k].astype(F32)
@@ -288,11 +292,16 @@
     grad[:, 32:64] = grad[:, 32:64] + mm(c[...], inflow).reshape(NH, 32, N)
     mate_send[...] = grad[...].astype(BF)
 
+    def owners(first):
+        turn = lax.div(first + 6, NH) * (NH - first)
+        return [ring(first + lax.rem(turn + i, 7)) for i in range(7)]
+
+    mine = owners(ring(z - 7 * (1 - odd) + odd))
+    mates = owners(ring(mate - 7 * odd + (1 - odd))) + [mate]
     mate_copies = []
-    for j in range(7, -1, -1):
-        rows = ring(mate - sgn * j)
+    for j in range(8):
         mate_copies.append(pltpu.make_async_remote_copy(
-            src_ref=mate_send.at[rows], dst_ref=mate_recv.at[j], send_sem=mt_ss.at[j], recv_sem=mt_rs.at[j],
+            src_ref=mate_send.at[mates[j]], dst_ref=mate_recv.at[j], send_sem=mt_ss.at[j], recv_sem=mt_rs.at[j],
             device_id={"head": mate}, device_id_type=MESH,
         ))
     for copy in mate_copies:
@@ -305,8 +314,8 @@
         ).wait_recv()
 
     back_copies = []
-    for j in range(7, 0, -1):
-        to = near_z[j - 1]
+    for j in range(7):
+        to = mine[j]
         mate_arrive(j)
         out_send[j] = (grad[to] + mate_recv[j].astype(F32)).astype(BF)
         copy = pltpu.make_async_remote_copy(
@@ -315,8 +324,8 @@
         )
         copy.start()
         back_copies.append(copy)
-    mate_arrive(0)
-    back[pair] = (grad[z] + mate_recv[0].astype(F32)).astype(BF)
+    mate_arrive(7)
+    back[pair] = (grad[z] + mate_recv[7].astype(F32)).astype(BF)
 
     stores = []
 
@@ -379,7 +388,6 @@
 
 def per_device(values, group_keys, group_queries, level_table, window_index, prior_states, cotangent):
     hbm = pl.BlockSpec(memory_space=pltpu.HBM)
-    smem = pl.BlockSpec(memory_space=pltpu.SMEM)
     dma = pltpu.SemaphoreType.DMA
     wide, narrow = jax.ShapeDtypeStruct((TOK, HP), BF), jax.ShapeDtypeStruct((256, N), F32)
     parts = pl.pallas_call(
@@ -389,9 +397,11 @@
             jax.ShapeDtypeStruct((NS, 16, N), BF),
             jax.ShapeDtypeStruct((32, N), F32),
         ),
-        in_specs=[hbm, hbm, hbm, smem, smem, hbm, hbm],
+        in_specs=[hbm] * 7,
         out_specs=(hbm,) * 6,
         scratch_shapes=[
+            pltpu.SMEM((LOC, 20), jnp.int32),
+            pltpu.SMEM((1,), jnp.int32),
             pltpu.VMEM((TOK, HP), BF),
             pltpu.VMEM((TOK, HP), BF),
             pltpu.VMEM((256, N), BF),
@@ -422,7 +432,7 @@
             pltpu.VMEM((2, TOK, HP), BF),
             pltpu.VMEM((2, 256, N), F32),
             pltpu.VMEM((32, N), F32),
-            dma((11,)),
+            dma((13,)),
             dma((GROUPS,)),
             dma((NH,)),
             dma((7,)),

time: 58.9 us -> 57.9 us (0.983)
  the two profiles are of different devices: /device:TPU:8 before, /device:TPU:32 now
where the time goes in v1:
time: 57.9 us; the launch traced here: 57.7 us
  Pallas kernels  56.4 us (97%)
  between operations  1.29 us (2%)
    pallas_call x1, Pallas kernels, per_device(): pl.pallas_call(kernel, out_shape=(wide, wide, narrow, narrow, jax.ShapeDt...  54 us
    pallas_call x1, Pallas kernels, per_device(): pl.pallas_call(store_kernel, out_shape=(wide, wide, narrow, narrow, jax.S...  2.44 us

profile of v1, /device:TPU:32, one launch (start us, length us, event | category | flops | bytes accessed | tf_op | source)
XLA Modules:
  0.0 57.7 jit_solution(10380191984117835382)
XLA Ops:
  1.3 54.0 %shard_map.110 = (bf16[512,512]{1,0:T(8,128)(2,1)}, bf16[512,512]{1,0:T(8,128)(2,1)}, f32[256,128]{1,0:T(8,128)}, f32[256,128]{1,0:T(8,128)}, bf16[32,16,128]{2,1,0:T(8,128)(2,1)}, /*index=5*/f32[32,128]{1,0:T(8,128)}) custom-call(bf16[512,512]{1,0:T(8,128)(2,1)} %v_hbm.1, bf16[256,128]{1,0:T(8,128)(2,1)} %bitcast.7, bf16[256,128]{1,0:T(8,128)(2,1)} %bitcast.8, ...), custom_call_target="tpu_custom_call" | custom-call | tf_op jit(solution)/shard_map/pallas_call | solution.py:393
  55.2 2.4 %shard_map.111 = (bf16[512,512]{1,0:T(8,128)(2,1)}, bf16[512,512]{1,0:T(8,128)(2,1)}, f32[256,128]{1,0:T(8,128)}, f32[256,128]{1,0:T(8,128)}, f32[4,512,128]{2,1,0:T(8,128)}) custom-call(bf16[512,512]{1,0:T(8,128)(2,1)} %get-tuple-element.16.refs_0_, bf16[512,512]{1,0:T(8,128)(2,1)} %get-tuple-element.17.refs_1_, f32[256,128]{1,0:T(8,128)} %get-tuple-element.18.refs_2_, ...), custom_call_target="tpu_custom_call" | custom-call | tf_op jit(solution)/shard_map/pallas_call | solution.py:462

commit v2 on v1

--- a/solution.py
+++ b/solution.py
@@ -42,9 +42,9 @@
     v_hbm, k_hbm, q_hbm, table_hbm, window_hbm, prior_hbm, c_hbm,
     mix_hbm, gv_hbm, gk_hbm, gq_hbm, tot_hbm, prior_w_hbm,
     table, window, v, c, kraw, qraw, prior, vt, ct, kq_send, kq, factor, factor_t,
-    g_diag, g_8, g_9, sa_send, sa_recv, io_send, io_recv, tot_send, tot_recv,
+    g_diag, g_8, g_9, sa_send, sa_recv, io_send, io_recv,
     mix, gval, grad, mate_send, mate_recv, out_send, back, outs, rows_out, prior_w,
-    local_sem, gat_send, gat_recv, fwd_send, sa_ss, sa_rs, io_ss, io_rs, tot_ss, tot_rs,
+    local_sem, gat_send, gat_recv, fwd_send, sa_ss, sa_rs, io_ss, io_rs,
     mt_ss, mt_rs, bk_ss, bk_rs,
 ):
     me = lax.axis_index("seq")
@@ -58,6 +58,7 @@
 
     def seq_of(rel):
         dy, dx, dc = rel
+        dy, dx = dy + core * ((4 - dy) % 4 - dy), dx + core * ((4 - dx) % 4 - dx)
         return lax.rem(yy + dy, 4) * 8 + lax.rem(xx + dx, 4) * 2 + lax.rem(core + dc, 2)
 
     relative = hops()
@@ -186,12 +187,12 @@
     sa_send[:, 0] = mm(vt[...], keys).astype(BF).reshape(NS, 16, N)
     sa_send[:, 1] = mm(ct[...], queries).astype(BF).reshape(NS, 16, N)
 
-    def spread_out(src, dst, ss, rs, whole):
+    def spread_out(src, dst, ss, rs):
         copies = []
         for n, rel in enumerate(relative):
             to = seq_of(rel)
             copies.append(pltpu.make_async_remote_copy(
-                src_ref=src if whole else src.at[to], dst_ref=dst.at[me], send_sem=ss.at[n], recv_sem=rs.at[me],
+                src_ref=src.at[to], dst_ref=dst.at[me], send_sem=ss.at[n], recv_sem=rs.at[me],
                 device_id={"seq": to}, device_id_type=MESH,
             ))
         for copy in copies:
@@ -206,7 +207,7 @@
                 device_id={"seq": frm}, device_id_type=MESH,
             ).wait_recv()
 
-    sa_copies = spread_out(sa_send, sa_recv, sa_ss, sa_rs, False)
+    sa_copies = spread_out(sa_send, sa_recv, sa_ss, sa_rs)
     sa_recv[me] = sa_send[me]
 
     def block(i):
@@ -276,12 +277,10 @@
         flow = [x for j, f in enumerate(flow) for x in (f + seq_w[b] * levels[b][2 * j + 1], f)]
     for j in range(NS):
         io_send[j, 1] = flow[j].astype(BF)
-    tot_send[...] = levels[5][0].astype(BF)
-
-    io_copies = spread_out(io_send, io_recv, io_ss, io_rs, False)
-    tot_copies = spread_out(tot_send, tot_recv, tot_ss, tot_rs, True)
+    io_send[:, 2] = jnp.broadcast_to(levels[5][0].astype(BF)[None], (32, 16, N))
+
+    io_copies = spread_out(io_send, io_recv, io_ss, io_rs)
     io_recv[me] = io_send[me]
-    tot_recv[me] = tot_send[...]
 
     inner_outputs()
 
@@ -341,8 +340,7 @@
         for k in range(4):
             prior_w[8 * k + h : 8 * k + h + 1, :] = jnp.full((1, N), weight(h, 15 + k) * bit(k), F32)
     store(prior_w, prior_w_hbm)
-    arrive(tot_recv, tot_ss, tot_rs)
-    store(tot_recv, tot_hbm)
+    store(io_recv.at[:, 2], tot_hbm)
 
     for k in range(1, 8):
         frm = lax.rem(pair + k, 8)
@@ -356,7 +354,7 @@
     store(rows_out.at[0], gk_hbm)
     store(rows_out.at[1], gq_hbm)
 
-    for copy in gathers + forwards + sa_copies + io_copies + tot_copies + mate_copies + back_copies:
+    for copy in gathers + forwards + sa_copies + io_copies + mate_copies + back_copies:
         copy.wait_send()
     for copy in stores:
         copy.wait()
@@ -418,10 +416,8 @@
             pltpu.VMEM((256, 256), BF),
             pltpu.VMEM((NS, 2, 16, N), BF),
             pltpu.VMEM((NS, 2, 16, N), BF),
-            pltpu.VMEM((NS, 2, 16, N), BF),
-            pltpu.VMEM((NS, 2, 16, N), BF),
-            pltpu.VMEM((16, N), BF),
-            pltpu.VMEM((NS, 16, N), BF),
+            pltpu.VMEM((NS, 3, 16, N), BF),
+            pltpu.VMEM((NS, 3, 16, N), BF),
             pltpu.VMEM((TOK, HP), F32),
             pltpu.VMEM((TOK, HP), F32),
             pltpu.VMEM((NH, 64, N), F32),
@@ -436,8 +432,6 @@
             dma((GROUPS,)),
             dma((NH,)),
             dma((7,)),
-            dma((NS,)),
-            dma((NS,)),
             dma((NS,)),
             dma((NS,)),
             dma((NS,)),

time: 57.9 us -> 57.6 us (level)
  no operation moved by 1% of the time
where the time goes in v2:
time: 57.6 us; the launch traced here: 57.4 us
  Pallas kernels  56.1 us (97%)
  between operations  1.29 us (2%)
    pallas_call x1, Pallas kernels, per_device(): pl.pallas_call(kernel, out_shape=(wide, wide, narrow, narrow, jax.ShapeDt...  53.7 us
    pallas_call x1, Pallas kernels, per_device(): pl.pallas_call(store_kernel, out_shape=(wide, wide, narrow, narrow, jax.S...  2.44 us

profile of v2, /device:TPU:32, one launch (start us, length us, event | category | flops | bytes accessed | tf_op | source)
XLA Modules:
  0.0 57.4 jit_solution(15994501619287049328)
XLA Ops:
  1.3 53.7 %shard_map.110 = (bf16[512,512]{1,0:T(8,128)(2,1)}, bf16[512,512]{1,0:T(8,128)(2,1)}, f32[256,128]{1,0:T(8,128)}, f32[256,128]{1,0:T(8,128)}, bf16[32,16,128]{2,1,0:T(8,128)(2,1)}, /*index=5*/f32[32,128]{1,0:T(8,128)}) custom-call(bf16[512,512]{1,0:T(8,128)(2,1)} %v_hbm.1, bf16[256,128]{1,0:T(8,128)(2,1)} %bitcast.7, bf16[256,128]{1,0:T(8,128)(2,1)} %bitcast.8, ...), custom_call_target="tpu_custom_call" | custom-call | tf_op jit(solution)/shard_map/pallas_call | solution.py:391
  55.0 2.4 %shard_map.111 = (bf16[512,512]{1,0:T(8,128)(2,1)}, bf16[512,512]{1,0:T(8,128)(2,1)}, f32[256,128]{1,0:T(8,128)}, f32[256,128]{1,0:T(8,128)}, f32[4,512,128]{2,1,0:T(8,128)}) custom-call(bf16[512,512]{1,0:T(8,128)(2,1)} %get-tuple-element.16.refs_0_, bf16[512,512]{1,0:T(8,128)(2,1)} %get-tuple-element.17.refs_1_, f32[256,128]{1,0:T(8,128)} %get-tuple-element.18.refs_2_, ...), custom_call_target="tpu_custom_call" | custom-call | tf_op jit(solution)/shard_map/pallas_call | solution.py:456
